TPU v7x, 512 devices: a whole 4x8x8 slice. The times are simulated.
512 devices in a mesh: panel: 32 (over z, x_lo, core), case: 16 (over x_hi, y).
Axes of the slice: x: 4 (x_hi: 2, x_lo: 2; x = x_hi * 2 + x_lo), y: 8, z: 8, core: 2. Of those that a mesh axis runs over, the one named last changes fastest.
Arguments:
- strengths: bfloat16 [32, 196608], P('panel', 'case'), may hold values from -6 to 6
- blocks: bfloat16 [16384, 256, 256], P(('panel', 'case')), may hold values from -0.109375 to 0.109375
- pattern: int32 [16384, 3], P(('panel', 'case')), may hold values from -1 to 767, as said below
- level_gain: float32 [8], replicated, may hold values from 0.25 to 2
Outputs:
- forward_one: bfloat16 [32, 196608], P('case', 'panel')
- adjoint_one: bfloat16 [32, 196608], P('panel', 'case')
- forward_two: bfloat16 [32, 196608], P('case', 'panel')
- adjoint_two: bfloat16 [32, 196608], P('panel', 'case')
Inputs may be any that keep to these rules, and one draw needn't show every extreme that they name: `pattern`: entries come in runs of 32, one run for each pair of a panel index p and a case index c, ordered with p slowest; a run's row blocks lie in p * 24 to (p + 1) * 24 - 1 and its column blocks in c * 48 to (c + 1) * 48 - 1; no (row block, column block) pair appears twice; levels lie in 0 to 7; an empty slot is (-1, -1, -1), a run holds its stored blocks first and its empty slots after them, every run holds at least one stored block and some run is full.
All inputs are finite; a program needn't handle non-finite values.
Results may differ from a plain program's by a relative error of at most 0.024.
Values may be sent and summed in bfloat16 or wider, within the bound.
A program may use at most 64 MiB of HBM per device.

v0:
```python
import contextlib

import jax
import jax.numpy as jnp
from jax import lax
from jax.experimental import pallas as pl
from jax.experimental.pallas import tpu as pltpu
from jax.sharding import PartitionSpec as P

B = 256
ROWB = 24
COLB = 48
BLK = 32
CASES = 32
LANES = 128
PART = 3
RING = 8
MESH = pl.DeviceIdType.MESH
FAR_FIRST = (4, 3, 5, 2, 6, 1, 7)
NEAR_FIRST = (1, 7, 2, 6, 3, 5, 4)

f32 = jnp.float32
bf16 = jnp.bfloat16


def chunk(ref, q, count=1):
    return ref.at[pl.ds(q * PART, count * PART)]


def read(ref, q):
    return ref[pl.ds(q * PART, PART)].astype(f32)


def stage(name):
    return contextlib.nullcontext()


class Link:
    def __init__(self, send_sem, recv_sem):
        self.send_sem, self.recv_sem = send_sem, recv_sem
        self.used = 0
        self.open = []

    def take(self, count):
        first = self.used
        self.used += count
        return first

    def copy(self, src, dst, slot_out, slot_in, device):
        return pltpu.make_async_remote_copy(
            src_ref=src,
            dst_ref=dst,
            send_sem=self.send_sem.at[slot_out],
            recv_sem=self.recv_sem.at[slot_in],
            device_id=device,
            device_id_type=MESH,
        )

    def send(self, src, dst, slot_out, slot_in, device):
        copy = self.copy(src, dst, slot_out, slot_in, device)
        copy.start()
        self.open.append(copy)

    def arrived(self, dst, slot_in, device):
        self.copy(dst, dst, slot_in, slot_in, device).wait_recv()

    def drain(self):
        for copy in self.open:
            copy.wait_send()
        self.open = []


class Group:
    def __init__(self, ring, pair, core=None):
        (self.i, self.peer), (self.j, self.partner) = ring, pair
        self.core, self.twin = core if core else (None, None)
        self.base = 0 if core is None else self.core * 16

    def at(self, d):
        return lax.rem(self.i + d, RING)


def gather(link, g, buf):
    own_ring = g.base + g.j * RING
    far_ring = g.base + (1 - g.j) * RING
    ring, pair = link.take(RING), link.take(RING)
    twin = link.take(2) if g.twin is not None else None
    mine = chunk(buf, own_ring + g.i)
    link.send(mine, mine, pair, pair, g.partner)
    for d in FAR_FIRST:
        link.send(mine, mine, ring + d, ring + RING - d, g.peer(d))
    for d in NEAR_FIRST:
        piece = chunk(buf, own_ring + g.at(d))
        link.arrived(piece, ring + d, g.peer(d))
        link.send(piece, piece, pair + d, pair + d, g.partner)
    if twin is not None:
        whole = chunk(buf, own_ring, RING)
        link.send(whole, whole, twin, twin, g.twin)
    for d in (0,) + NEAR_FIRST:
        link.arrived(chunk(buf, far_ring + g.at(d)), pair + d, g.partner)
    if twin is not None:
        whole = chunk(buf, far_ring, RING)
        link.send(whole, whole, twin + 1, twin + 1, g.twin)
        other = (1 - g.core) * 16
        link.arrived(chunk(buf, other + g.j * RING, RING), twin, g.twin)
        link.arrived(chunk(buf, other + (1 - g.j) * RING, RING), twin + 1, g.twin)


def scatter(link, g, src, from_twin, joined, from_pair, summed, from_ring):
    if g.twin is not None:
        slots = link.take(2)
        other = (1 - g.core) * 16
        for n, half in enumerate((1 - g.j, g.j)):
            link.send(
                chunk(src, other + half * RING, RING),
                chunk(from_twin, half * RING, RING),
                slots + n,
                slots + n,
                g.twin,
            )

        def join(half):
            def one(t, carry):
                at = half * RING * PART + t
                joined[at] = (
                    src[g.base * PART + at].astype(f32) + from_twin[at].astype(f32)
                ).astype(bf16)
                return carry

            lax.fori_loop(0, RING * PART, one, 0)

        link.arrived(chunk(from_twin, (1 - g.j) * RING, RING), slots, g.twin)
        join(1 - g.j)
    ready = src if g.twin is None else joined
    pair, ring = link.take(RING), link.take(RING)
    far, near = (1 - g.j) * RING, g.j * RING
    for d in FAR_FIRST + (0,):
        link.send(chunk(ready, far + g.at(d)), chunk(from_pair, d), pair + d, pair + d, g.partner)
    if g.twin is not None:
        link.arrived(chunk(from_twin, g.j * RING, RING), slots + 1, g.twin)
        join(g.j)
    for d in FAR_FIRST:
        link.arrived(chunk(from_pair, d), pair + d, g.partner)
        total = read(ready, near + g.at(d)) + read(from_pair, d)
        summed[pl.ds(d * PART, PART)] = total.astype(bf16)
        link.send(
            chunk(summed, d), chunk(from_ring, RING - d), ring + d, ring + RING - d, g.peer(d)
        )
    link.arrived(chunk(from_pair, 0), pair, g.partner)
    total = read(ready, near + g.i) + read(from_pair, 0)
    for d in NEAR_FIRST:
        link.arrived(chunk(from_ring, d), ring + d, g.peer(d))
        total = total + read(from_ring, d)
    return total


def kernel(
    table, scale, strengths, blocks_hbm,
    fwd_one, adj_one, fwd_two, adj_two,
    blocks, rows_in, x_one, x_two, f_one, f_two, y_one, y_two, z_one, z_two,
    terms, wide, flat, twin_buf, join_buf, pair_buf, sum_buf, ring_buf,
    send_sem, recv_sem, load_sem,
):
    p, c = lax.axis_index("panel"), lax.axis_index("case")
    z, x_lo, core = p // 4, lax.rem(p // 2, 2), lax.rem(p, 2)
    x_hi, y = c // RING, lax.rem(c, RING)
    load = pltpu.make_async_copy(blocks_hbm, blocks, load_sem)
    load.start()

    by_panel = Group(
        (z, lambda d: {"panel": lax.rem(z + d, RING) * 4 + x_lo * 2 + core}),
        (x_lo, {"panel": z * 4 + (1 - x_lo) * 2 + core}),
        (core, {"panel": z * 4 + x_lo * 2 + (1 - core)}),
    )
    by_case = Group(
        (y, lambda d: {"case": x_hi * RING + lax.rem(y + d, RING)}),
        (x_hi, {"case": (1 - x_hi) * RING + y}),
    )
    barrier = pltpu.get_barrier_semaphore()
    met = [by_panel.twin, by_panel.partner, by_case.partner]
    met += [g.peer(d) for d in NEAR_FIRST for g in (by_panel, by_case)]
    for device in met:
        pl.semaphore_signal(barrier, inc=1, device_id=device, device_id_type=MESH)

    place = core * 16 + x_lo * RING + z

    for n in range(COLB * 2):
        flat[n : n + 1, :] = strengths[0:1, n * LANES : (n + 1) * LANES].astype(f32)
    for n in range(PART):
        rows_in[place * PART + n] = flat[n * CASES : (n + 1) * CASES, :].astype(bf16)
    terms[BLK] = jnp.zeros((CASES, B), f32)
    with stage("meet"):
        pl.semaphore_wait(barrier, len(met))

    link = Link(send_sem, recv_sem)
    with stage("gath0"):
        gather(link, by_panel, rows_in)

    def widen(t, carry):
        wide[pl.ds(t * CASES, CASES), :] = rows_in[t].astype(f32)
        return carry

    lax.fori_loop(0, COLB * 2, widen, 0)

    def turn(t, carry):
        x_one[t] = wide[pl.ds(t, CASES, stride=COLB * 2), :].astype(bf16)
        return carry

    lax.fori_loop(0, COLB * 2, turn, 0)
    with stage("load"):
        load.wait()

    def product(src, where_from, chained, dims):
        def some(step, carry):
            found = []
            for n in range(4):
                b = step * 4 + n
                at = table[where_from + b] * 2
                operand = jnp.concatenate([src[at], src[at + 1]], axis=1)
                found.append(
                    lax.dot_general(operand, blocks[b], (dims, ((), ())), preferred_element_type=f32)
                    * scale[b]
                )
            for n in range(4):
                b = step * 4 + n
                terms[b] = found[n] + terms[table[chained + b]]
            return carry

        lax.fori_loop(0, BLK // 4, some, 0)

    def forward(src, dst):
        product(src, BLK, 2 * BLK, ((1,), (1,)))

        def out(r, carry):
            total = terms[table[4 * BLK + r]].astype(bf16)
            dst[2 * r] = total[:, :LANES]
            dst[2 * r + 1] = total[:, LANES:]
            return carry

        lax.fori_loop(0, ROWB, out, 0)

    def adjoint(src, dst):
        product(src, 0, 3 * BLK, ((1,), (0,)))

        def out(r, carry):
            total = terms[table[4 * BLK + ROWB + r]]
            if dst is None:
                wide[pl.ds(2 * r, CASES, stride=COLB * 2), :] = total[:, :LANES]
                wide[pl.ds(2 * r + 1, CASES, stride=COLB * 2), :] = total[:, LANES:]
            else:
                total = total.astype(bf16)
                dst[2 * r] = total[:, :LANES]
                dst[2 * r + 1] = total[:, LANES:]
            return carry

        lax.fori_loop(0, COLB, out, 0)

    def pick(src, dst, places, count):
        lane = lax.broadcasted_iota(jnp.int32, (8, CASES), 1)
        line = lax.broadcasted_iota(jnp.int32, (8, CASES), 0)
        chosen = jnp.zeros((8, CASES), f32)
        for n, at in enumerate(places):
            chosen = jnp.where((line == n) & (lane == at), f32(1.0), chosen)
        chosen = chosen.astype(bf16)
        for t in range(count):
            both = jnp.concatenate([src[2 * t], src[2 * t + 1]], axis=1)
            found = jnp.dot(chosen, both, preferred_element_type=f32)
            dst[:, t * B : (t + 1) * B] = found[: len(places)].astype(bf16)

    def place_of(k):
        return lax.rem(k, 2) * 16 + lax.rem(k // 2, 2) * RING + k // 4

    mine = [place_of(2 * c), place_of(2 * c + 1)]

    def reduce_rows(n, src, dst):
        with stage("rs"):
            total = scatter(
                link, by_case, src, None, None, pair_buf.at[n], sum_buf.at[n], ring_buf.at[n]
            )
        with stage("ag"):
            dst[pl.ds(c * PART, PART)] = total.astype(bf16)
            gather(link, by_case, dst)

    with stage("fwd1"):
        forward(x_one, y_one)
    with stage("red1"):
        reduce_rows(0, y_one, f_one)
    with stage("adj1"):
        adjoint(f_one, z_one)
        pick(f_one, fwd_one, mine, ROWB)
    with stage("scat2"):
        total = scatter(
            link, by_panel, z_one, twin_buf.at[0], join_buf.at[0],
            pair_buf.at[1], sum_buf.at[1], ring_buf.at[1],
        )
    with stage("gath2"):
        x_two[pl.ds(place * PART, PART)] = total.astype(bf16)
        gather(link, by_panel, x_two)
    with stage("fwd2"):
        forward(x_two, y_two)
    with stage("red3"):
        reduce_rows(2, y_two, f_two)
    with stage("adj2"):
        adjoint(f_two, None)

        def narrow(t, carry):
            z_two[t] = wide[pl.ds(t * CASES, CASES), :].astype(bf16)
            return carry

        lax.fori_loop(0, COLB * 2, narrow, 0)
        pick(x_two, adj_one, [place], COLB)
        pick(f_two, fwd_two, mine, ROWB)
    with stage("scat4"):
        total = scatter(
            link, by_panel, z_two, twin_buf.at[1], join_buf.at[1],
            pair_buf.at[3], sum_buf.at[3], ring_buf.at[3],
        )
    for n in range(PART):
        flat[n * CASES : (n + 1) * CASES, :] = total[n]
    for n in range(COLB * 2):
        adj_two[0:1, n * LANES : (n + 1) * LANES] = flat[n : n + 1, :].astype(bf16)
    link.drain()


COPIES = 160


def tables(pattern, level_gain):
    level_ids = jnp.arange(level_gain.shape[0], dtype=jnp.int32)
    scale = jnp.sum(
        jnp.where(pattern[:, 2:3] == level_ids[None, :], level_gain[None, :], f32(0.0)), axis=1
    )
    live = pattern[:, 2] >= 0
    row = jnp.where(live, pattern[:, 0] - lax.axis_index("panel") * ROWB, -1)
    col = jnp.where(live, pattern[:, 1] - lax.axis_index("case") * COLB, -1)
    slot = jnp.arange(BLK, dtype=jnp.int32)

    def last(keys, own, before):
        hit = own[:, None] == keys[None, :]
        if before:
            hit = hit & (slot[None, :] < slot[:, None])
        found = jnp.max(jnp.where(hit, slot[None, :], -1), axis=1)
        return jnp.where(found < 0, BLK, found)

    table = jnp.concatenate([
        jnp.maximum(row, 0),
        jnp.maximum(col, 0),
        last(row, row, True),
        last(col, col, True),
        last(row, jnp.arange(ROWB, dtype=jnp.int32), False),
        last(col, jnp.arange(COLB, dtype=jnp.int32), False),
    ])
    return table, scale


def shards(strengths, blocks, pattern, level_gain):
    table, scale = tables(pattern, level_gain)
    V = pltpu.VMEM
    cols = (2 * COLB, CASES, LANES)
    rows = (2 * ROWB, CASES, LANES)
    ring = (RING * PART, CASES, LANES)
    half = (2, 2 * RING * PART, CASES, LANES)
    return pl.pallas_call(
        kernel,
        out_shape=(
            jax.ShapeDtypeStruct((2, ROWB * B), bf16),
            jax.ShapeDtypeStruct((1, COLB * B), bf16),
            jax.ShapeDtypeStruct((2, ROWB * B), bf16),
            jax.ShapeDtypeStruct((1, COLB * B), bf16),
        ),
        in_specs=[
            pl.BlockSpec(memory_space=pltpu.SMEM),
            pl.BlockSpec(memory_space=pltpu.SMEM),
            pl.BlockSpec(memory_space=pltpu.VMEM),
            pl.BlockSpec(memory_space=pl.ANY),
        ],
        out_specs=tuple(pl.BlockSpec(memory_space=pltpu.VMEM) for _ in range(4)),
        scratch_shapes=[
            V((BLK, B, B), bf16),
            V(cols, bf16), V(cols, bf16), V(cols, bf16),
            V(rows, bf16), V(rows, bf16), V(rows, bf16), V(rows, bf16),
            V(cols, bf16), V(cols, bf16),
            V((BLK + 1, CASES, B), f32),
            V((2 * COLB * CASES, LANES), f32),
            V((2 * COLB, LANES), f32),
            V(half, bf16), V(half, bf16),
            V((4, *ring), bf16), V((4, *ring), bf16), V((4, *ring), bf16),
            pltpu.SemaphoreType.DMA((COPIES,)),
            pltpu.SemaphoreType.DMA((COPIES,)),
            pltpu.SemaphoreType.DMA,
        ],
        compiler_params=pltpu.CompilerParams(
            collective_id=0, has_side_effects=True, vmem_limit_bytes=40 << 20
        ),
    )(table, scale, strengths, blocks)


def solution(mesh):
    in_specs = (
        P("panel", "case"),
        P(("panel", "case"), None, None),
        P(("panel", "case"), None),
        P(),
    )
    out_specs = (P("case", "panel"), P("panel", "case"), P("case", "panel"), P("panel", "case"))
    return jax.shard_map(shards, mesh=mesh, in_specs=in_specs, out_specs=out_specs, check_vma=False)
```

profile of v0, /device:TPU:1, one launch (start us, length us, event | category | flops | bytes accessed | tf_op | source)
XLA Modules:
  0.0 132.4 jit_solution(18340459244018948922)
XLA Ops:
  0.6 0.8 slice_bitcast_fusion
  1.4 0.7 select_reduce_fusion.4.scale
  2.2 0.8 broadcast_maximum_fusion
  3.0 0.2 select_reduce_fusion.1
  3.2 0.1 select_reduce_fusion.3
  3.3 0.1 select_reduce_fusion
  3.4 0.1 concatenate.3.table
  3.5 0.0 copy-start
  3.5 2.2 %copy-done = bf16[32,256,256]{2,1,0:T(8,128)(2,1)S(1)} copy-done((bf16[32,256,256]{2,1,0:T(8,128)(2,1)S(1)}, bf16[32,256,256]{2,1,0:T(8,128)(2,1)}, u32[]{:S(2)}) %copy-start) | copy-done | bytes 4194328
  5.7 0.0 copy-start.1
  5.7 0.8 copy-done.1
  6.5 123.5 %shard_map.75 = (bf16[2,6144]{1,0:T(2,128)(2,1)S(1)}, bf16[1,12288]{1,0:T(2,128)(2,1)S(1)}, bf16[2,6144]{1,0:T(2,128)(2,1)S(1)}, bf16[1,12288]{1,0:T(2,128)(2,1)S(1)}) custom-call(s32[200]{0:T(256)S(1)} %concatenate.3.table, f32[32]{0:T(128)S(1)} %select_reduce_fusion.4.scale, bf16[1,12288]{1,0:T(2,128)(2,1)S(1)} %copy-done.1, bf16[32,256,256]{2,1,0:T(8,128)(2,1)S(1)} %copy-done), custom_call_target="tpu_custom_call" | custom-call | tf_op jit(solution)/shard_map/pallas_call | solution.py:363
  130.0 0.6 copy.12
  130.6 0.6 copy.13
  131.2 0.6 copy.14
  131.8 0.6 copy.15
  (4 shorter events, 0.0 us)
Async XLA Ops:
  3.5 2.2 %copy-start = (bf16[32,256,256]{2,1,0:T(8,128)(2,1)S(1)}, bf16[32,256,256]{2,1,0:T(8,128)(2,1)}, u32[]{:S(2)}) copy-start(bf16[32,256,256]{2,1,0:T(8,128)(2,1)} %blocks_hbm.1) | copy-start | bytes 12582916
  5.7 0.8 copy-start.1
where the time goes:
time: 133 us; the launch traced here: 132 us
  Pallas kernels  123 us (92%)
  local copies, waits for them, and re-layouts  5.52 us (4%)
  other arithmetic  2.75 us (2%)
    pallas_call x1, Pallas kernels, shards(): pl.pallas_call(kernel, out_shape=(jax.ShapeDtypeStruct((2, ROWB * B), bf1...  123 us
    unnamed x8, local copies, waits for them, and re-layouts  5.44 us

commit v1 on v0

v1 whole, which is shorter than its diff:
```python
import jax
import jax.numpy as jnp
from jax import lax
from jax.experimental import pallas as pl
from jax.experimental.pallas import tpu as pltpu
from jax.sharding import PartitionSpec as P

B = 256
ROWB = 24
COLB = 48
BLK = 32
CASES = 32
LANES = 128
PART = 3
RING = 8
MESH = pl.DeviceIdType.MESH
FAR_FIRST = (4, 3, 5, 2, 6, 1, 7)
NEAR_FIRST = (1, 7, 2, 6, 3, 5, 4)

f32 = jnp.float32
bf16 = jnp.bfloat16


def chunk(ref, q, count=1):
    return ref.at[pl.ds(q * PART, count * PART)]


def read(ref, q):
    return ref[pl.ds(q * PART, PART)].astype(f32)


def repeat(count, body, unroll=8):
    def some(step, carry):
        for n in range(unroll):
            body(step * unroll + n)
        return carry

    lax.fori_loop(0, count // unroll, some, 0)


class Link:
    def __init__(self, send_sem, recv_sem):
        self.send_sem, self.recv_sem = send_sem, recv_sem
        self.used = 0
        self.open = []

    def take(self, count):
        first = self.used
        self.used += count
        return first

    def copy(self, src, dst, slot_out, slot_in, device):
        return pltpu.make_async_remote_copy(
            src_ref=src,
            dst_ref=dst,
            send_sem=self.send_sem.at[slot_out],
            recv_sem=self.recv_sem.at[slot_in],
            device_id=device,
            device_id_type=MESH,
        )

    def send(self, src, dst, slot_out, slot_in, device):
        copy = self.copy(src, dst, slot_out, slot_in, device)
        copy.start()
        self.open.append(copy)

    def arrived(self, dst, slot_in, device):
        self.copy(dst, dst, slot_in, slot_in, device).wait_recv()

    def drain(self):
        for copy in self.open:
            copy.wait_send()
        self.open = []


class Group:
    def __init__(self, ring, pair, core=None):
        (self.i, self.peer), (self.j, self.partner) = ring, pair
        self.core, self.twin = core if core else (None, None)
        self.base = 0 if core is None else self.core * 16

    def at(self, d):
        return lax.rem(self.i + d, RING)


def gather(link, g, buf, meanwhile=None):
    own_ring = g.base + g.j * RING
    far_ring = g.base + (1 - g.j) * RING
    ring, pair = link.take(RING), link.take(RING)
    twin = link.take(2) if g.twin is not None else None
    mine = chunk(buf, own_ring + g.i)
    link.send(mine, mine, pair, pair, g.partner)
    for d in NEAR_FIRST:
        link.send(mine, mine, ring + d, ring + RING - d, g.peer(d))
    if meanwhile is not None:
        meanwhile()
    for d in NEAR_FIRST:
        piece = chunk(buf, own_ring + g.at(d))
        link.arrived(piece, ring + d, g.peer(d))
        link.send(piece, piece, pair + d, pair + d, g.partner)
    if twin is not None:
        whole = chunk(buf, own_ring, RING)
        link.send(whole, whole, twin, twin, g.twin)
    for d in (0,) + NEAR_FIRST:
        link.arrived(chunk(buf, far_ring + g.at(d)), pair + d, g.partner)
    if twin is not None:
        whole = chunk(buf, far_ring, RING)
        link.send(whole, whole, twin + 1, twin + 1, g.twin)
        other = (1 - g.core) * 16
        link.arrived(chunk(buf, other + g.j * RING, RING), twin, g.twin)
        link.arrived(chunk(buf, other + (1 - g.j) * RING, RING), twin + 1, g.twin)


def scatter(link, g, src, from_twin, joined, from_pair, summed, from_ring, ready_half=None, meanwhile=None):
    if g.twin is not None:
        slots = link.take(2)
        other = (1 - g.core) * 16
        for n, half in enumerate((1 - g.j, g.j)):
            if ready_half is not None:
                ready_half((other + half * RING) * PART)
            link.send(
                chunk(src, other + half * RING, RING),
                chunk(from_twin, half * RING, RING),
                slots + n,
                slots + n,
                g.twin,
            )

        def join(half):
            def one(t):
                at = half * RING * PART + t
                joined[at] = (
                    src[g.base * PART + at].astype(f32) + from_twin[at].astype(f32)
                ).astype(bf16)

            repeat(RING * PART, one)

        if ready_half is not None:
            ready_half((g.base + (1 - g.j) * RING) * PART)
            ready_half((g.base + g.j * RING) * PART)
        link.arrived(chunk(from_twin, (1 - g.j) * RING, RING), slots, g.twin)
        join(1 - g.j)
    ready = src if g.twin is None else joined
    pair, ring = link.take(RING), link.take(RING)
    far, near = (1 - g.j) * RING, g.j * RING
    for d in FAR_FIRST + (0,):
        link.send(chunk(ready, far + g.at(d)), chunk(from_pair, d), pair + d, pair + d, g.partner)
    if g.twin is not None:
        link.arrived(chunk(from_twin, g.j * RING, RING), slots + 1, g.twin)
        join(g.j)
    if meanwhile is not None:
        meanwhile()
    for d in FAR_FIRST:
        link.arrived(chunk(from_pair, d), pair + d, g.partner)
        total = read(ready, near + g.at(d)) + read(from_pair, d)
        summed[pl.ds(d * PART, PART)] = total.astype(bf16)
        link.send(
            chunk(summed, d), chunk(from_ring, RING - d), ring + d, ring + RING - d, g.peer(d)
        )
    link.arrived(chunk(from_pair, 0), pair, g.partner)
    total = read(ready, near + g.i) + read(from_pair, 0)
    for d in NEAR_FIRST:
        link.arrived(chunk(from_ring, d), ring + d, g.peer(d))
        total = total + read(from_ring, d)
    return total


def kernel(
    strengths_hbm, blocks_hbm, pattern_hbm, gain_hbm,
    fwd_one, adj_one, fwd_two, adj_two,
    blocks, rows_in, x_one, x_two, f_one, f_two, y_one, y_two, z_one, z_two,
    terms, wide, flat, twin_buf, join_buf, pair_buf, sum_buf, ring_buf,
    strengths, pattern, pattern_at, gain, keys, found_at, scale_row, table, scale,
    send_sem, recv_sem, load_sem,
):
    p, c = lax.axis_index("panel"), lax.axis_index("case")
    z, x_lo, core = p // 4, lax.rem(p // 2, 2), lax.rem(p, 2)
    x_hi, y = c // RING, lax.rem(c, RING)

    by_panel = Group(
        (z, lambda d: {"panel": lax.rem(z + d, RING) * 4 + x_lo * 2 + core}),
        (x_lo, {"panel": z * 4 + (1 - x_lo) * 2 + core}),
        (core, {"panel": z * 4 + x_lo * 2 + (1 - core)}),
    )
    by_case = Group(
        (y, lambda d: {"case": x_hi * RING + lax.rem(y + d, RING)}),
        (x_hi, {"case": (1 - x_hi) * RING + y}),
    )
    barrier = pltpu.get_barrier_semaphore()
    met = [g.peer(d) for d in (4, 3, 5, 2, 6, 1, 7) for g in (by_panel, by_case)]
    met += [by_panel.twin, by_panel.partner, by_case.partner]
    for device in met:
        pl.semaphore_signal(barrier, inc=1, device_id=device, device_id_type=MESH)

    loads = [
        pltpu.make_async_copy(src, dst, load_sem.at[n])
        for n, (src, dst) in enumerate((
            (strengths_hbm, strengths),
            (pattern_hbm, pattern),
            (pattern_hbm, pattern_at),
            (gain_hbm, gain),
            (blocks_hbm, blocks),
        ))
    ]
    for load in loads:
        load.start()
    place = core * 16 + x_lo * RING + z
    terms[BLK] = jnp.zeros((CASES, B), f32)

    loads[0].wait()
    for n in range(COLB * 2):
        flat[n : n + 1, :] = strengths[0:1, n * LANES : (n + 1) * LANES].astype(f32)
    for n in range(PART):
        rows_in[place * PART + n] = flat[n * CASES : (n + 1) * CASES, :].astype(bf16)
    for load in loads[1:4]:
        load.wait()
    pl.semaphore_wait(barrier, len(met))

    def index_tables():
        line = lax.broadcasted_iota(jnp.int32, (8, LANES), 0)
        lane = lax.broadcasted_iota(jnp.int32, (8, LANES), 1)
        keys[...] = lane
        keys[0:1, 0:BLK] = pattern[0:1, :] - p * ROWB
        keys[1:2, 0:BLK] = pattern[1:2, :] - c * COLB
        wanted = keys[...]
        until = jnp.where(line < 2, lane, BLK)
        by_row = (line == 0) | (line == 2)
        last = jnp.full((8, LANES), BLK, jnp.int32)
        for b in range(BLK):
            live = pattern_at[2, b] >= 0
            row = jnp.where(live, pattern_at[0, b] - p * ROWB, -1000)
            col = jnp.where(live, pattern_at[1, b] - c * COLB, -1000)
            hit = (wanted == jnp.where(by_row, row, col)) & (until > b)
            last = jnp.where(hit, b, last)
        found_at[...] = last
        found_at[4:5, 0:BLK] = jnp.maximum(wanted[0:1, 0:BLK], 0)
        found_at[5:6, 0:BLK] = jnp.maximum(wanted[1:2, 0:BLK], 0)
        chosen = jnp.zeros((1, BLK), f32)
        for n in range(gain_hbm.shape[1]):
            chosen = jnp.where(pattern[2:3, :] == n, gain[0, n], chosen)
        scale_row[0:1, 0:BLK] = chosen
        to_scalars = [
            pltpu.make_async_copy(found_at, table, load_sem.at[0]),
            pltpu.make_async_copy(scale_row, scale, load_sem.at[1]),
        ]
        for copy in to_scalars:
            copy.start()
        for copy in to_scalars:
            copy.wait()

    link = Link(send_sem, recv_sem)
    gather(link, by_panel, rows_in, index_tables)

    def widen(t):
        wide[pl.ds(t * CASES, CASES), :] = rows_in[t].astype(f32)

    def turn(t):
        x_one[t] = wide[pl.ds(t, CASES, stride=COLB * 2), :].astype(bf16)

    repeat(COLB * 2, widen)
    repeat(COLB * 2, turn)
    loads[4].wait()

    def product(src, where_from, chained, dims, unroll):
        def some(step, carry):
            found = []
            for n in range(unroll):
                b = step * unroll + n
                at = table[where_from, b] * 2
                operand = jnp.concatenate([src[at], src[at + 1]], axis=1)
                found.append(
                    lax.dot_general(operand, blocks[b], (dims, ((), ())), preferred_element_type=f32)
                    * scale[0, b]
                )
            for n in range(unroll):
                b = step * unroll + n
                terms[b] = found[n] + terms[table[chained, b]]
            return carry

        lax.fori_loop(0, BLK // unroll, some, 0)

    def forward(src, dst):
        product(src, 5, 0, ((1,), (1,)), 8)

        def out(r):
            total = terms[table[2, r]].astype(bf16)
            dst[2 * r] = total[:, :LANES]
            dst[2 * r + 1] = total[:, LANES:]

        repeat(ROWB, out)

    def adjoint(src, dst):
        product(src, 4, 1, ((1,), (0,)), 16)

        def out(r):
            total = terms[table[3, r]]
            if dst is None:
                wide[pl.ds(2 * r, CASES, stride=COLB * 2), :] = total[:, :LANES]
                wide[pl.ds(2 * r + 1, CASES, stride=COLB * 2), :] = total[:, LANES:]
            else:
                total = total.astype(bf16)
                dst[2 * r] = total[:, :LANES]
                dst[2 * r + 1] = total[:, LANES:]

        repeat(COLB, out)

    def pick(src, dst, places, count):
        lane = lax.broadcasted_iota(jnp.int32, (8, CASES), 1)
        line = lax.broadcasted_iota(jnp.int32, (8, CASES), 0)
        chosen = jnp.zeros((8, CASES), f32)
        for n, at in enumerate(places):
            chosen = jnp.where((line == n) & (lane == at), f32(1.0), chosen)
        chosen = chosen.astype(bf16)
        for t in range(count):
            both = jnp.concatenate([src[2 * t], src[2 * t + 1]], axis=1)
            found = jnp.dot(chosen, both, preferred_element_type=f32)
            dst[:, t * B : (t + 1) * B] = found[: len(places)].astype(bf16)

    def place_of(k):
        return lax.rem(k, 2) * 16 + lax.rem(k // 2, 2) * RING + k // 4

    mine = [place_of(2 * c), place_of(2 * c + 1)]

    def reduce_rows(n, src, dst, meanwhile=None):
        total = scatter(
            link, by_case, src, None, None, pair_buf.at[n], sum_buf.at[n], ring_buf.at[n],
            meanwhile=meanwhile,
        )
        dst[pl.ds(c * PART, PART)] = total.astype(bf16)
        gather(link, by_case, dst)

    def reduce_cols(n, src, ready_half, meanwhile):
        return scatter(
            link, by_panel, src, twin_buf.at[n], join_buf.at[n],
            pair_buf.at[2 * n + 1], sum_buf.at[2 * n + 1], ring_buf.at[2 * n + 1],
            ready_half=ready_half, meanwhile=meanwhile,
        )

    forward(x_one, y_one)
    reduce_rows(0, y_one, f_one)
    adjoint(f_one, z_one)
    total = reduce_cols(0, z_one, None, lambda: pick(f_one, fwd_one, mine, ROWB))
    x_two[pl.ds(place * PART, PART)] = total.astype(bf16)
    gather(link, by_panel, x_two)
    forward(x_two, y_two)
    reduce_rows(2, y_two, f_two, lambda: pick(x_two, adj_one, [place], COLB))
    adjoint(f_two, None)

    def narrow(first):
        def one(t):
            z_two[first + t] = wide[pl.ds((first + t) * CASES, CASES), :].astype(bf16)

        repeat(RING * PART, one)

    total = reduce_cols(1, z_two, narrow, lambda: pick(f_two, fwd_two, mine, ROWB))
    for n in range(PART):
        flat[n * CASES : (n + 1) * CASES, :] = total[n]
    for n in range(COLB * 2):
        adj_two[0:1, n * LANES : (n + 1) * LANES] = flat[n : n + 1, :].astype(bf16)
    link.drain()


COPIES = 160
GRANT = 40 << 20


def shards(strengths, blocks, pattern, level_gain):
    V = pltpu.VMEM
    cols = (2 * COLB, CASES, LANES)
    rows = (2 * ROWB, CASES, LANES)
    ring = (RING * PART, CASES, LANES)
    half = (2, 2 * RING * PART, CASES, LANES)
    results = pl.pallas_call(
        kernel,
        out_shape=(
            jax.ShapeDtypeStruct((2, ROWB * B), bf16),
            jax.ShapeDtypeStruct((1, COLB * B), bf16),
            jax.ShapeDtypeStruct((2, ROWB * B), bf16),
            jax.ShapeDtypeStruct((1, COLB * B), bf16),
        ),
        in_specs=[pl.BlockSpec(memory_space=pltpu.HBM)] * 4,
        out_specs=tuple(pl.BlockSpec(memory_space=pltpu.VMEM) for _ in range(4)),
        scratch_shapes=[
            V((BLK, B, B), bf16),
            V(cols, bf16), V(cols, bf16), V(cols, bf16),
            V(rows, bf16), V(rows, bf16), V(rows, bf16), V(rows, bf16),
            V(cols, bf16), V(cols, bf16),
            V((BLK + 1, CASES, B), f32),
            V((2 * COLB * CASES, LANES), f32),
            V((2 * COLB, LANES), f32),
            V(half, bf16), V(half, bf16),
            V((4, *ring), bf16), V((4, *ring), bf16), V((4, *ring), bf16),
            V((1, COLB * B), bf16),
            V((3, BLK), jnp.int32),
            pltpu.SMEM((3, BLK), jnp.int32),
            pltpu.SMEM((1, level_gain.shape[0]), f32),
            V((8, LANES), jnp.int32), V((8, LANES), jnp.int32), V((8, LANES), f32),
            pltpu.SMEM((8, LANES), jnp.int32), pltpu.SMEM((8, LANES), f32),
            pltpu.SemaphoreType.DMA((COPIES,)),
            pltpu.SemaphoreType.DMA((COPIES,)),
            pltpu.SemaphoreType.DMA((5,)),
        ],
        compiler_params=pltpu.CompilerParams(
            collective_id=0, has_side_effects=True, vmem_limit_bytes=GRANT
        ),
    )(*(pltpu.with_memory_space_constraint(a, pltpu.HBM) for a in (strengths, blocks, pattern.T, level_gain[None, :])))

    def hand_over(*refs):
        ins, outs, sem = refs[:4], refs[4:8], refs[8]
        copies = [pltpu.make_async_copy(a, b, sem.at[n]) for n, (a, b) in enumerate(zip(ins, outs))]
        for copy in copies:
            copy.start()
        for copy in copies:
            copy.wait()

    return pl.pallas_call(
        hand_over,
        out_shape=tuple(jax.ShapeDtypeStruct(r.shape, r.dtype) for r in results),
        in_specs=[pl.BlockSpec(memory_space=pltpu.VMEM)] * 4,
        out_specs=tuple(pl.BlockSpec(memory_space=pl.ANY) for _ in results),
        scratch_shapes=[pltpu.SemaphoreType.DMA((4,))],
    )(*(pltpu.with_memory_space_constraint(r, pltpu.VMEM) for r in results))


def solution(mesh):
    in_specs = (
        P("panel", "case"),
        P(("panel", "case"), None, None),
        P(("panel", "case"), None),
        P(),
    )
    out_specs = (P("case", "panel"), P("panel", "case"), P("case", "panel"), P("panel", "case"))
    return jax.shard_map(shards, mesh=mesh, in_specs=in_specs, out_specs=out_specs, check_vma=False)
```

time: 133 us -> 114 us (0.86)
  Pallas kernels: 123 us -> 113 us
  local copies, waits for them, and re-layouts: 5.52 us -> 0 us
  other arithmetic: 2.75 us -> 0 us
    pallas_call x1, Pallas kernels: 123 us -> 112 us  [shards(): pl.pallas_call(kernel, out_shape=(jax.ShapeDtypeStruct((2, ROWB * B), bf1...]
    unnamed x8 -> x0, local copies, waits for them, and re-layouts: 5.44 us -> none
where the time goes in v1:
time: 114 us; the launch traced here: 113 us
  Pallas kernels  113 us (99%)
    pallas_call x1, Pallas kernels, shards(): pl.pallas_call(kernel, out_shape=(jax.ShapeDtypeStruct((2, ROWB * B), bf1...  112 us

profile of v1, /device:TPU:1, one launch (start us, length us, event | category | flops | bytes accessed | tf_op | source)
XLA Modules:
  0.0 113.3 jit_solution(18241064506254783676)
XLA Ops:
  0.6 112.0 %shard_map.75 = (bf16[2,6144]{1,0:T(2,128)(2,1)S(1)}, bf16[1,12288]{1,0:T(2,128)(2,1)S(1)}, bf16[2,6144]{1,0:T(2,128)(2,1)S(1)}, bf16[1,12288]{1,0:T(2,128)(2,1)S(1)}) custom-call(bf16[1,12288]{1,0:T(2,128)(2,1)} %strengths_hbm.1, bf16[32,256,256]{2,1,0:T(8,128)(2,1)} %blocks_hbm.1, s32[3,32]{1,0:T(4,128)} %bitcast.2, f32[1,8]{1,0:T(1,128)} %bitcast.3), custom_call_target="tpu_custom_call" | custom-call | tf_op jit(solution)/shard_map/pallas_call | solution.py:373
  112.6 0.7 shard_map.76

commit v2 on v1

--- a/solution.py
+++ b/solution.py
@@ -83,11 +83,11 @@
         return lax.rem(self.i + d, RING)
 
 
-def gather(link, g, buf, meanwhile=None):
+def gather(link, g, buf, meanwhile=None, before_last=None):
     own_ring = g.base + g.j * RING
     far_ring = g.base + (1 - g.j) * RING
     ring, pair = link.take(RING), link.take(RING)
-    twin = link.take(2) if g.twin is not None else None
+    twin = link.take(1 + RING) if g.twin is not None else None
     mine = chunk(buf, own_ring + g.i)
     link.send(mine, mine, pair, pair, g.partner)
     for d in NEAR_FIRST:
@@ -102,13 +102,18 @@
         whole = chunk(buf, own_ring, RING)
         link.send(whole, whole, twin, twin, g.twin)
     for d in (0,) + NEAR_FIRST:
-        link.arrived(chunk(buf, far_ring + g.at(d)), pair + d, g.partner)
+        piece = chunk(buf, far_ring + g.at(d))
+        link.arrived(piece, pair + d, g.partner)
+        if twin is not None:
+            link.send(piece, piece, twin + 1 + d, twin + 1 + d, g.twin)
+    if before_last is not None:
+        before_last()
     if twin is not None:
-        whole = chunk(buf, far_ring, RING)
-        link.send(whole, whole, twin + 1, twin + 1, g.twin)
         other = (1 - g.core) * 16
         link.arrived(chunk(buf, other + g.j * RING, RING), twin, g.twin)
-        link.arrived(chunk(buf, other + (1 - g.j) * RING, RING), twin + 1, g.twin)
+        for d in (0,) + NEAR_FIRST:
+            piece = chunk(buf, other + (1 - g.j) * RING + g.at(d))
+            link.arrived(piece, twin + 1 + d, g.twin)
 
 
 def scatter(link, g, src, from_twin, joined, from_pair, summed, from_ring, ready_half=None, meanwhile=None):
@@ -168,7 +173,7 @@
 def kernel(
     strengths_hbm, blocks_hbm, pattern_hbm, gain_hbm,
     fwd_one, adj_one, fwd_two, adj_two,
-    blocks, rows_in, x_one, x_two, f_one, f_two, y_one, y_two, z_one, z_two,
+    blocks, turned, rows_in, x_one, x_two, f_one, f_two, y_one, y_two, z_one, z_two,
     terms, wide, flat, twin_buf, join_buf, pair_buf, sum_buf, ring_buf,
     strengths, pattern, pattern_at, gain, keys, found_at, scale_row, table, scale,
     send_sem, recv_sem, load_sem,
@@ -245,23 +250,34 @@
         ]
         for copy in to_scalars:
             copy.start()
+        loads[4].wait()
+
+        def turn_block(b):
+            turned[b] = blocks[b].T
+
+        repeat(BLK, turn_block, 1)
         for copy in to_scalars:
             copy.wait()
 
+    def turn_rows(first):
+        first = pl.multiple_of(first, 16)
+
+        def widen(t):
+            at = first * PART + t
+            wide[pl.ds(at * CASES, CASES), :] = rows_in[at].astype(f32)
+
+        def turn(t):
+            found = wide[pl.ds(first * COLB * 2 + t, 16, stride=COLB * 2), :]
+            x_one[t, pl.ds(first, 16), :] = found.astype(bf16)
+
+        repeat(16 * PART, widen)
+        repeat(COLB * 2, turn)
+
     link = Link(send_sem, recv_sem)
-    gather(link, by_panel, rows_in, index_tables)
-
-    def widen(t):
-        wide[pl.ds(t * CASES, CASES), :] = rows_in[t].astype(f32)
-
-    def turn(t):
-        x_one[t] = wide[pl.ds(t, CASES, stride=COLB * 2), :].astype(bf16)
-
-    repeat(COLB * 2, widen)
-    repeat(COLB * 2, turn)
-    loads[4].wait()
-
-    def product(src, where_from, chained, dims, unroll):
+    gather(link, by_panel, rows_in, index_tables, lambda: turn_rows(core * 16))
+    turn_rows((1 - core) * 16)
+
+    def product(src, where_from, chained, tiles, unroll=16):
         def some(step, carry):
             found = []
             for n in range(unroll):
@@ -269,8 +285,7 @@
                 at = table[where_from, b] * 2
                 operand = jnp.concatenate([src[at], src[at + 1]], axis=1)
                 found.append(
-                    lax.dot_general(operand, blocks[b], (dims, ((), ())), preferred_element_type=f32)
-                    * scale[0, b]
+                    jnp.dot(operand, tiles[b], preferred_element_type=f32) * scale[0, b]
                 )
             for n in range(unroll):
                 b = step * unroll + n
@@ -280,7 +295,7 @@
         lax.fori_loop(0, BLK // unroll, some, 0)
 
     def forward(src, dst):
-        product(src, 5, 0, ((1,), (1,)), 8)
+        product(src, 5, 0, turned)
 
         def out(r):
             total = terms[table[2, r]].astype(bf16)
@@ -290,7 +305,7 @@
         repeat(ROWB, out)
 
     def adjoint(src, dst):
-        product(src, 4, 1, ((1,), (0,)), 16)
+        product(src, 4, 1, blocks)
 
         def out(r):
             total = terms[table[3, r]]
@@ -381,7 +396,7 @@
         in_specs=[pl.BlockSpec(memory_space=pltpu.HBM)] * 4,
         out_specs=tuple(pl.BlockSpec(memory_space=pltpu.VMEM) for _ in range(4)),
         scratch_shapes=[
-            V((BLK, B, B), bf16),
+            V((BLK, B, B), bf16), V((BLK, B, B), bf16),
             V(cols, bf16), V(cols, bf16), V(cols, bf16),
             V(rows, bf16), V(rows, bf16), V(rows, bf16), V(rows, bf16),
             V(cols, bf16), V(cols, bf16),

time: 114 us -> 112 us (0.982)
  Pallas kernels: 113 us -> 111 us
    pallas_call x1, Pallas kernels: 112 us -> 110 us  [shards(): pl.pallas_call(kernel, out_shape=(jax.ShapeDtypeStruct((2, ROWB * B), bf1...]
where the time goes in v2:
time: 112 us; the launch traced here: 111 us
  Pallas kernels  111 us (99%)
    pallas_call x1, Pallas kernels, shards(): pl.pallas_call(kernel, out_shape=(jax.ShapeDtypeStruct((2, ROWB * B), bf1...  110 us

profile of v2, /device:TPU:1, one launch (start us, length us, event | category | flops | bytes accessed | tf_op | source)
XLA Modules:
  0.0 111.5 jit_solution(3750511493609464304)
XLA Ops:
  0.6 110.2 %shard_map.75 = (bf16[2,6144]{1,0:T(2,128)(2,1)S(1)}, bf16[1,12288]{1,0:T(2,128)(2,1)S(1)}, bf16[2,6144]{1,0:T(2,128)(2,1)S(1)}, bf16[1,12288]{1,0:T(2,128)(2,1)S(1)}) custom-call(bf16[1,12288]{1,0:T(2,128)(2,1)} %strengths_hbm.1, bf16[32,256,256]{2,1,0:T(8,128)(2,1)} %blocks_hbm.1, s32[3,32]{1,0:T(4,128)} %bitcast.2, f32[1,8]{1,0:T(1,128)} %bitcast.3), custom_call_target="tpu_custom_call" | custom-call | tf_op jit(solution)/shard_map/pallas_call | solution.py:388
  110.8 0.7 shard_map.76

commit v3 on v2

--- a/solution.py
+++ b/solution.py
@@ -16,6 +16,7 @@
 MESH = pl.DeviceIdType.MESH
 FAR_FIRST = (4, 3, 5, 2, 6, 1, 7)
 NEAR_FIRST = (1, 7, 2, 6, 3, 5, 4)
+FAR = (4, 3, 5)
 
 f32 = jnp.float32
 bf16 = jnp.bfloat16
@@ -94,16 +95,26 @@
         link.send(mine, mine, ring + d, ring + RING - d, g.peer(d))
     if meanwhile is not None:
         meanwhile()
-    for d in NEAR_FIRST:
+    for d in NEAR_FIRST[:2]:
         piece = chunk(buf, own_ring + g.at(d))
         link.arrived(piece, ring + d, g.peer(d))
         link.send(piece, piece, pair + d, pair + d, g.partner)
+    across = chunk(buf, far_ring + g.i)
+    link.arrived(across, pair, g.partner)
+    for d in FAR:
+        link.send(across, across, pair + d, pair + RING - d, g.peer(d))
+    for d in NEAR_FIRST[2:]:
+        piece = chunk(buf, own_ring + g.at(d))
+        link.arrived(piece, ring + d, g.peer(d))
+        if d not in FAR:
+            link.send(piece, piece, pair + d, pair + d, g.partner)
     if twin is not None:
         whole = chunk(buf, own_ring, RING)
         link.send(whole, whole, twin, twin, g.twin)
-    for d in (0,) + NEAR_FIRST:
+        link.send(across, across, twin + 1, twin + 1, g.twin)
+    for d in NEAR_FIRST:
         piece = chunk(buf, far_ring + g.at(d))
-        link.arrived(piece, pair + d, g.partner)
+        link.arrived(piece, pair + d, g.peer(d) if d in FAR else g.partner)
         if twin is not None:
             link.send(piece, piece, twin + 1 + d, twin + 1 + d, g.twin)
     if before_last is not None:

time: 112 us -> 111 us (level)
  no operation moved by 1% of the time
where the time goes in v3:
time: 111 us
  Pallas kernels  110 us (99%)
    pallas_call x1, Pallas kernels, shards(): pl.pallas_call(kernel, out_shape=(jax.ShapeDtypeStruct((2, ROWB * B), bf1...  110 us

profile of v3, /device:TPU:1, one launch (start us, length us, event | category | flops | bytes accessed | tf_op | source)
XLA Modules:
  0.0 111.0 jit_solution(15244121177916307114)
XLA Ops:
  0.6 109.7 %shard_map.75 = (bf16[2,6144]{1,0:T(2,128)(2,1)S(1)}, bf16[1,12288]{1,0:T(2,128)(2,1)S(1)}, bf16[2,6144]{1,0:T(2,128)(2,1)S(1)}, bf16[1,12288]{1,0:T(2,128)(2,1)S(1)}) custom-call(bf16[1,12288]{1,0:T(2,128)(2,1)} %strengths_hbm.1, bf16[32,256,256]{2,1,0:T(8,128)(2,1)} %blocks_hbm.1, s32[3,32]{1,0:T(4,128)} %bitcast.2, f32[1,8]{1,0:T(1,128)} %bitcast.3), custom_call_target="tpu_custom_call" | custom-call | tf_op jit(solution)/shard_map/pallas_call | solution.py:399
  110.3 0.7 shard_map.76
